TPU v7x, 512 devices: a whole 4x8x8 slice. The times are simulated.
512 devices in a mesh: seq: 32 (over y, x), chan: 16 (over z, core).
Axes of the slice: x: 4, y: 8, z: 8, core: 2. Of those that a mesh axis runs over, the one named last changes fastest.
Arguments:
- tokens: bfloat16 [8192, 2048], P(('seq', 'chan')), may hold values from -6 to 6
- norm_gain: float32 [2048], replicated, may hold values from 0.1 to 1.9
- entry_projection_matrix: bfloat16 [2, 2048, 4096], P(None, None, 'chan'), may hold values from -0.125 to 0.125
- conv_weight: float32 [4, 4096], P(None, 'chan'), may hold values from -3 to 3
- conv_bias: float32 [4096], P('chan'), may hold values from -3 to 3
- w_x: bfloat16 [4096, 160], P('chan'), may hold values from -0.09375 to 0.09375
- timescale_matrix: bfloat16 [128, 4096], P(None, 'chan'), may hold values from -0.5 to 0.5
- timescale_offset: float32 [4096], P('chan'), may hold values from -8 to -2
- a_log: float32 [16, 4096], P(None, 'chan'), may hold values from -1 to 2.77
- skip_gain: float32 [4096], P('chan'), may hold values from 0.5 to 1.5
- w_out: bfloat16 [4096, 2048], P('chan'), may hold values from -0.09375 to 0.09375
- lengths: int32 [4], replicated, may hold values from 1 to 4096, 7936 in all
- req_order: int32 [4], replicated, may hold values from 0 to 3, each once
Outputs:
- mixed: bfloat16 [8192, 2048], P(('seq', 'chan'))
- last_states: float32 [4, 16, 4096], P(None, None, ('chan', 'seq'))
- conv_edges: bfloat16 [4, 4, 4096], P(None, None, ('chan', 'seq'))
Inputs may be any that keep to these rules, and one draw needn't show every extreme that they name: The lengths sum to exactly 7936, and the longest is exactly 4096. `req_order`: each request appears exactly once.
All inputs are finite; a program needn't handle non-finite values.
Results may differ from a plain program's by a relative error of at most 0.0095.
Values may be sent and summed in bfloat16 or wider, within the bound.
No kernel may reach another device: no remote copies, remote signals or barrier semaphores. Data moves between devices by JAX's collectives and lax.ppermute only.
A program may use at most 64 MiB of HBM per device.

v0:
```python
import jax
import jax.numpy as jnp
from jax import lax
from jax.sharding import PartitionSpec as P

STRETCH = 64


def shifted(block, axis, distance):
    devices = range(lax.axis_size(axis))
    route = [(i - distance, i) for i in devices if i - distance in devices]
    return lax.ppermute(block, axis, route)


def sequence_arrangement(lengths, req_order, slot_ids):
    req_count = lengths.shape[0]
    req_index = jnp.arange(req_count, dtype=jnp.int32)
    filled_length_total = (lengths + STRETCH - 1) // STRETCH * STRETCH
    pick_order = (req_order[:, None] == req_index[None, :]).astype(jnp.int32)
    placed_pad = jnp.sum(pick_order * filled_length_total[None, :], axis=1)
    placed_len = jnp.sum(pick_order * lengths[None, :], axis=1)
    end_slots = jnp.cumsum(placed_pad)
    begin_slots = end_slots - placed_pad
    sequence_beginnings = jnp.sum(pick_order * begin_slots[:, None], axis=0)
    inside = (slot_ids[:, None] >= begin_slots[None, :]) & (slot_ids[:, None] < end_slots[None, :])
    slot_owner = jnp.sum(jnp.where(inside, req_index[None, :] + 1, 0), axis=1)
    slot_owner = jnp.where(slot_ids < 0, -1, slot_owner)
    in_request = inside & (slot_ids[:, None] - begin_slots[None, :] < placed_len[None, :])
    present_flag = jnp.sum(jnp.where(in_request, 1, 0), axis=1).astype(jnp.int32)
    return (filled_length_total, sequence_beginnings, slot_owner, present_flag)


def chain_pair(earlier, later):
    return (earlier[0] * later[0], later[0] * earlier[1] + later[1])


def on_device(
    tokens,
    norm_gain,
    entry_projection_matrix,
    conv_weight,
    conv_bias,
    w_x,
    timescale_matrix,
    timescale_offset,
    a_log,
    skip_gain,
    w_out,
    lengths,
    req_order,
):
    tok_rows = tokens.shape[0]
    seq_rows = tok_rows * lax.axis_size("chan")
    chan_width = entry_projection_matrix.shape[2]
    state_size = a_log.shape[0]
    rank_size = timescale_matrix.shape[0]
    halo_count = conv_weight.shape[0] - 1
    req_count = lengths.shape[0]
    base_slot = lax.axis_index("seq") * seq_rows
    ext_slots = base_slot - halo_count + jnp.arange(seq_rows + halo_count, dtype=jnp.int32)
    filled_length_total, sequence_beginnings, padded_request_owner, widened_presence_mask = (
        sequence_arrangement(lengths, req_order, ext_slots)
    )
    slot_owner = padded_request_owner[halo_count:]
    position_presence = widened_presence_mask[halo_count:].astype(jnp.float32)
    widened = tokens.astype(jnp.float32)
    scale_row = lax.rsqrt(jnp.mean(widened * widened, axis=1, keepdims=True) + 1e-05)
    rescaled_entries = (widened * scale_row * norm_gain[None, :]).astype(jnp.bfloat16)
    mapped_signal = jnp.einsum(
        "td,kde->kte",
        lax.all_gather(rescaled_entries, "chan", axis=0, tiled=True),
        entry_projection_matrix,
        preferred_element_type=jnp.float32,
    )
    mixer_signal = (mapped_signal[0] * position_presence[:, None]).astype(jnp.bfloat16)
    switch_signal = mapped_signal[1].astype(jnp.bfloat16)
    rim_rows = shifted(mixer_signal[seq_rows - halo_count :], "seq", 1)
    extended = jnp.concatenate([rim_rows, mixer_signal], axis=0).astype(jnp.float32)
    conv_sum = conv_bias[None, :] + jnp.zeros((seq_rows, chan_width), jnp.float32)
    for shift_by in range(halo_count + 1):
        lower = halo_count - shift_by
        same_req = (padded_request_owner[lower : lower + seq_rows] == slot_owner).astype(
            jnp.float32
        )
        conv_sum = (
            conv_sum
            + conv_weight[lower][None, :] * extended[lower : lower + seq_rows] * same_req[:, None]
        )
    activated = jax.nn.silu(conv_sum).astype(jnp.bfloat16)
    x_proj = lax.psum(jnp.dot(activated, w_x, preferred_element_type=jnp.float32), "chan")
    thin_timescale_factor = x_proj[:, :rank_size].astype(jnp.bfloat16)
    in_coef = x_proj[:, rank_size : rank_size + state_size]
    out_coef = x_proj[:, rank_size + state_size :]
    timescale_values = position_presence[:, None] * jax.nn.softplus(
        jnp.dot(thin_timescale_factor, timescale_matrix, preferred_element_type=jnp.float32)
        + timescale_offset[None, :]
    )
    decay_rate = -jnp.exp(a_log)
    keep_flag = (
        padded_request_owner[halo_count - 1 : halo_count - 1 + seq_rows] == slot_owner
    ).astype(jnp.float32)
    act_wide = activated.astype(jnp.float32)
    block_len = min(16, STRETCH)
    block_count = seq_rows // block_len

    def arrange(values):
        return jnp.swapaxes(values.reshape((block_count, block_len) + values.shape[1:]), 0, 1)

    def advance(running, slot_in):
        state_now, decay_now = running
        step_delta, step_input, step_in, step_out, step_keep = slot_in
        factor = step_keep[:, None, None] * jnp.exp(step_delta[:, None, :] * decay_rate[None])
        state_now = factor * state_now + (step_delta * step_input)[:, None, :] * step_in[:, :, None]
        decay_now = factor * decay_now
        local_out = jnp.sum(step_out[:, :, None] * state_now, axis=1)
        return ((state_now, decay_now), (local_out, step_out[:, :, None] * decay_now))

    empty_state = jnp.zeros((block_count, state_size, chan_width), jnp.float32)
    slot_in = (
        arrange(timescale_values),
        arrange(act_wide),
        arrange(in_coef),
        arrange(out_coef),
        arrange(keep_flag),
    )
    (block_state, block_decay), (local_y, weighted) = lax.scan(
        advance, (empty_state, jnp.ones_like(empty_state)), slot_in
    )
    incl_decay, incl_state = lax.associative_scan(chain_pair, (block_decay, block_state), axis=0)
    own_decay = incl_decay[-1]
    own_state = incl_state[-1]

    def relay(relay_turn, incoming):
        return shifted(own_decay * incoming + own_state, "seq", 1)

    incoming = lax.fori_loop(0, lax.axis_size("seq") - 1, relay, jnp.zeros_like(own_state))
    start_decay = jnp.concatenate([jnp.ones_like(incl_decay[:1]), incl_decay[:-1]], axis=0)
    start_state = jnp.concatenate([jnp.zeros_like(incl_state[:1]), incl_state[:-1]], axis=0)
    begin_state = start_decay * incoming[None] + start_state
    end_state = incl_decay * incoming[None] + incl_state
    carried = jnp.sum(weighted * begin_state[None], axis=2)
    complete_result = (
        jnp.swapaxes(local_y + carried, 0, 1).reshape(seq_rows, chan_width)
        + skip_gain[None, :] * act_wide
    )
    switched_result = (
        position_presence[:, None]
        * complete_result
        * jax.nn.silu(switch_signal.astype(jnp.float32))
    ).astype(jnp.bfloat16)
    summed = lax.psum_scatter(
        jnp.dot(switched_result, w_out, preferred_element_type=jnp.float32),
        "chan",
        scatter_dimension=0,
        tiled=True,
    )
    mixed = (widened + summed).astype(jnp.bfloat16)
    block_ends = base_slot + (jnp.arange(block_count, dtype=jnp.int32) + 1) * block_len - 1
    final_hits = (
        (sequence_beginnings + filled_length_total - 1)[:, None] == block_ends[None, :]
    ).astype(jnp.float32)
    state_part = jnp.einsum("rb,bne->rne", final_hits, end_state, precision=lax.Precision.HIGHEST)
    slots_here = base_slot + jnp.arange(seq_rows, dtype=jnp.int32)
    offsets = jnp.arange(halo_count + 1, dtype=jnp.int32)
    back_pos = lengths[:, None] - (halo_count + 1) + offsets[None, :]
    target = sequence_beginnings[:, None] + back_pos
    picked = (target[:, :, None] == slots_here[None, None, :]) & (back_pos >= 0)[:, :, None]
    pick_matrix = picked.astype(jnp.bfloat16).reshape(req_count * (halo_count + 1), seq_rows)
    edge_part = jnp.dot(pick_matrix, mixer_signal, preferred_element_type=jnp.float32).reshape(
        req_count, halo_count + 1, chan_width
    )
    last_states, edge_sums = (
        lax.psum_scatter(state_part, "seq", scatter_dimension=2, tiled=True),
        lax.psum_scatter(edge_part, "seq", scatter_dimension=2, tiled=True),
    )
    return (mixed, last_states, edge_sums.astype(jnp.bfloat16))


def solution(mesh):
    in_specs = (
        P(("seq", "chan"), None),
        P(),
        P(None, None, "chan"),
        P(None, "chan"),
        P("chan"),
        P("chan", None),
        P(None, "chan"),
        P("chan"),
        P(None, "chan"),
        P("chan"),
        P("chan", None),
        P(),
        P(),
    )
    out_specs = (
        P(("seq", "chan"), None),
        P(None, None, ("chan", "seq")),
        P(None, None, ("chan", "seq")),
    )
    return jax.shard_map(
        on_device, mesh=mesh, in_specs=in_specs, out_specs=out_specs, check_vma=False
    )
```

profile of v0, /device:TPU:4, one launch (start us, length us, event | category | flops | bytes accessed | tf_op | source)
XLA Modules:
  0.0 755.7 jit_solution(17366890487351695271)
XLA Ops:
  8.4 1.6 fusion.22
  14.9 42.3 %all-gather.2.cloned.1.call-done = bf16[256,2048]{1,0:T(8,128)(2,1)} async-done(((bf16[16,2048]{1,0:T(8,128)(2,1)}), bf16[256,2048]{1,0:T(8,128)(2,1)}) %all-gather.2.cloned.1.call-update) | async-done | bytes 1048592 | tf_op jit(solution)/shard_map/all_gather | solution.py:71
  57.3 1.9 convolution_bitcast_fusion
  60.1 3.1 collective-permute-start.1
  63.9 1.7 collective-permute-done.1
  68.1 107.0 %all-reduce.23.cloned.1.call-done = f32[256,160]{0,1:T(8,128)} async-done(((f32[256,160]{0,1:T(8,128)}), f32[256,160]{0,1:T(8,128)}) %all-reduce.23.cloned.1.call-update) | async-done | bytes 163856 | tf_op jit(solution)/shard_map/psum | solution.py:90
  178.4 49.3 %while.28 = (s32[]{:T(128)}, f32[16,16,256]{2,1,0:T(8,128)S(1)}, f32[16,16,256]{2,1,0:T(8,128)S(1)}, f32[16,16,256]{2,1,0:T(8,128)}, f32[16,16,16,256]{3,2,1,0:T...) while((s32[]{:T(128)}, f32[16,16,256]{2,1,0:T(8,128)S(1)}, ...), condition=%wide.region_9.10_spmd.clone, body=%wide.region_7.9_spmd.clone.sunk | while | flops 851971 | bytes 1532312 | solution.py:126
  234.5 2.9 pad.59
  237.5 1.6 pad_maximum_fusion
  239.0 2.9 pad.58
  242.7 234.2 %while.27 = (s32[]{:T(128)}, f32[16,256]{1,0:T(8,128)S(1)}, f32[16,256]{1,0:T(8,128)S(1)}, f32[16,256]{1,0:T(8,128)S(1)}, s32[]{:T(128)}) while((s32[]{:T(128)}, f32[16,256]{1,0:T(8,128)S(1)}, f32[16,256]{1,0:T(8,128)S(1)}, f32[16,256]{1,0:T(8,128)S(1)}, s32[]{:T(128)}) %tuple.80), condition=%wide.region_11.12_spmd, body=%wide.region_10.11_spmd.sunk | while | flops 8194 | bytes 131173 | solution.py:136
  242.7 3.1 collective-permute-start
  245.8 2.5 collective-permute-done
  248.3 3.1 collective-permute-start
  251.4 2.5 collective-permute-done
  254.0 4.4 collective-permute-start
  258.3 1.4 collective-permute-done
  259.8 6.3 collective-permute-start
  266.1 1.4 collective-permute-done
  267.5 6.3 collective-permute-start
  275.2 6.3 collective-permute-start
  281.6 1.4 collective-permute-done
  283.0 6.3 collective-permute-start
  289.3 1.4 collective-permute-done
  290.7 6.4 collective-permute-start
  297.1 1.4 collective-permute-done
  298.5 6.3 collective-permute-start
  306.3 6.3 collective-permute-start
  312.6 1.4 collective-permute-done
  314.0 6.3 collective-permute-start
  320.3 1.4 collective-permute-done
  321.7 6.3 collective-permute-start
  328.1 1.4 collective-permute-done
  329.5 6.3 collective-permute-start
  335.8 1.4 collective-permute-done
  337.2 6.5 collective-permute-start
  345.1 6.3 collective-permute-start
  351.4 1.4 collective-permute-done
  352.9 6.3 collective-permute-start
  359.2 1.4 collective-permute-done
  360.6 6.3 collective-permute-start
  366.9 1.4 collective-permute-done
  368.3 6.3 collective-permute-start
  374.6 1.4 collective-permute-done
  376.1 6.3 collective-permute-start
  383.8 6.4 collective-permute-start
  390.3 1.4 collective-permute-done
  391.7 6.3 collective-permute-start
  399.4 6.3 collective-permute-start
  407.2 6.3 collective-permute-start
  414.9 6.3 collective-permute-start
  422.6 6.3 collective-permute-start
  430.4 6.4 collective-permute-start
  438.2 6.3 collective-permute-start
  446.0 6.3 collective-permute-start
  453.7 6.3 collective-permute-start
  461.5 6.3 collective-permute-start
  469.2 6.3 collective-permute-start
  478.2 3.4 multiply_reduce_fusion.1
  485.4 1.8 fusion.54
  491.7 161.0 %all-reduce.19 = bf16[4,4,256]{2,1,0:T(4,128)(2,1)S(1)} all-reduce(f32[4,4,256]{2,1,0:T(4,128)S(1)} %fusion.25), channel_id=4, replica_groups=mesh['seq'=32,'chan'=16] {'seq'}, use_global_device_ids=true, to_apply=%region_16.17.clone | all-reduce | flops 4096 | bytes 24576
  653.4 29.1 %all-reduce.25.cloned.1.call-done = f32[4,16,256]{1,0,2:T(4,128)} async-done(((f32[4,16,256]{1,0,2:T(4,128)}), f32[4,16,256]{1,0,2:T(4,128)}) %all-reduce.25.cloned.1.call-update) | async-done | bytes 65552
  683.8 63.7 %reduce-scatter.3.cloned.1.call-done = f32[16,2048]{1,0:T(8,128)} async-done(((f32[256,2048]{1,0:T(8,128)}), f32[16,2048]{1,0:T(8,128)}) %reduce-scatter.3.cloned.1.call-update) | async-done | bytes 131088 | tf_op jit(solution)/shard_map/reduce_scatter | solution.py:151
  747.6 1.6 fusion.23
  (288 shorter events, 102.1 us)
Async XLA Ops:
  7.2 50.1 %copy-start = (bf16[2,2048,256]{2,1,0:T(8,128)(2,1)S(1)}, bf16[2,2048,256]{2,1,0:T(8,128)(2,1)}, u32[]{:S(2)}) copy-start(bf16[2,2048,256]{2,1,0:T(8,128)(2,1)} %param.19) | copy-start | bytes 6291460
  7.2 58.4 %copy-start.12 = (f32[256]{0:T(256)S(1)}, f32[256]{0:T(256)}, u32[]{:S(2)}) copy-start(f32[256]{0:T(256)} %param.21) | copy-start | bytes 3076
  7.2 58.7 %copy-start.5 = (bf16[256,160]{0,1:T(8,128)(2,1)S(1)}, bf16[256,160]{0,1:T(8,128)(2,1)}, u32[]{:S(2)}) copy-start(bf16[256,160]{0,1:T(8,128)(2,1)} %param.22) | copy-start | bytes 245764
  7.2 167.9 %copy-start.16 = (bf16[128,256]{1,0:T(8,128)(2,1)S(1)}, bf16[128,256]{1,0:T(8,128)(2,1)}, u32[]{:S(2)}) copy-start(bf16[128,256]{1,0:T(8,128)(2,1)} %param.23) | copy-start | bytes 196612
  7.2 167.9 %copy-start.17 = (f32[256]{0:T(256)S(1)}, f32[256]{0:T(256)}, u32[]{:S(2)}) copy-start(f32[256]{0:T(256)} %param.24) | copy-start | bytes 3076
  7.2 50.0 %all-gather.2.cloned.1.call-start = ((), (), s32[]{:S(2)}) async-start(), calls=%async_computation.1 | async-start | bytes 1114112 | tf_op jit(solution)/shard_map/all_gather | solution.py:71
  10.0 165.1 %all-reduce.23.cloned.1.call-start = ((), (), s32[]{:S(2)}) async-start(), calls=%async_computation.2 | async-start | bytes 327680 | tf_op jit(solution)/shard_map/psum | solution.py:90
  13.1 164.3 %copy-start.13 = (s32[4]{0:T(128)}, s32[4]{0:T(128)S(1)}, u32[]{:S(2)}) copy-start(s32[4]{0:T(128)S(1)} %get-tuple-element.173) | copy-start | bytes 52
  13.3 163.0 %copy-start.6 = (f32[256]{0:T(256)}, f32[256]{0:T(256)S(1)}, u32[]{:S(2)}) copy-start(f32[256]{0:T(256)S(1)} %get-tuple-element.237) | copy-start | bytes 3076
  13.3 163.0 %copy-start.7 = (f32[256]{0:T(256)}, f32[256]{0:T(256)S(1)}, u32[]{:S(2)}) copy-start(f32[256]{0:T(256)S(1)} %get-tuple-element.238) | copy-start | bytes 3076
  14.2 162.2 %copy-start.8 = (f32[1,256]{1,0:T(1,128)}, f32[1,256]{1,0:T(1,128)S(1)}, u32[]{:S(2)}) copy-start(f32[1,256]{1,0:T(1,128)S(1)} %get-tuple-element.233) | copy-start | bytes 3076
  14.2 162.2 %copy-start.9 = (f32[1,256]{1,0:T(1,128)}, f32[1,256]{1,0:T(1,128)S(1)}, u32[]{:S(2)}) copy-start(f32[1,256]{1,0:T(1,128)S(1)} %get-tuple-element.234) | copy-start | bytes 3076
  14.2 162.2 %copy-start.10 = (f32[1,256]{1,0:T(1,128)}, f32[1,256]{1,0:T(1,128)S(1)}, u32[]{:S(2)}) copy-start(f32[1,256]{1,0:T(1,128)S(1)} %get-tuple-element.235) | copy-start | bytes 3076
  14.2 162.2 %copy-start.11 = (f32[1,256]{1,0:T(1,128)}, f32[1,256]{1,0:T(1,128)S(1)}, u32[]{:S(2)}) copy-start(f32[1,256]{1,0:T(1,128)S(1)} %get-tuple-element.236) | copy-start | bytes 3076
  59.2 0.8 copy-start.2
  60.1 5.5 collective-permute-start.1
  66.8 615.7 %all-reduce.25.cloned.1.call-start = ((), (), s32[]{:S(2)}) async-start(), calls=%async_computation.4 | async-start | bytes 1048576
  242.7 5.6 collective-permute-start
  248.3 5.6 collective-permute-start
  254.0 5.8 collective-permute-start
  259.8 7.7 %collective-permute-start = (f32[16,256]{1,0:T(8,128)S(1)}, f32[16,256]{1,0:T(8,128)S(1)}, u32[]{:S(2)}, u32[]{:S(2)}) collective-permute-start(f32[16,256]{1,0:T(8,128)S(1)} %multiply_add_fusion.3), channel_id=1, source_target_pairs={{0,16},{16,32},{32,48},{48,64},{64,80},{80,96},{96,112},{112,128},... | collective-permute-start | bytes 49160 | tf_op jit(solution)/shard_map/while/body/eval_jaxpr/ppermute | solution.py:12
  267.5 7.7 %collective-permute-start = (f32[16,256]{1,0:T(8,128)S(1)}, f32[16,256]{1,0:T(8,128)S(1)}, u32[]{:S(2)}, u32[]{:S(2)}) collective-permute-start(f32[16,256]{1,0:T(8,128)S(1)} %multiply_add_fusion.3), channel_id=1, source_target_pairs={{0,16},{16,32},{32,48},{48,64},{64,80},{80,96},{96,112},{112,128},... | collective-permute-start | bytes 49160 | tf_op jit(solution)/shard_map/while/body/eval_jaxpr/ppermute | solution.py:12
  275.2 7.7 %collective-permute-start = (f32[16,256]{1,0:T(8,128)S(1)}, f32[16,256]{1,0:T(8,128)S(1)}, u32[]{:S(2)}, u32[]{:S(2)}) collective-permute-start(f32[16,256]{1,0:T(8,128)S(1)} %multiply_add_fusion.3), channel_id=1, source_target_pairs={{0,16},{16,32},{32,48},{48,64},{64,80},{80,96},{96,112},{112,128},... | collective-permute-start | bytes 49160 | tf_op jit(solution)/shard_map/while/body/eval_jaxpr/ppermute | solution.py:12
  283.0 7.7 %collective-permute-start = (f32[16,256]{1,0:T(8,128)S(1)}, f32[16,256]{1,0:T(8,128)S(1)}, u32[]{:S(2)}, u32[]{:S(2)}) collective-permute-start(f32[16,256]{1,0:T(8,128)S(1)} %multiply_add_fusion.3), channel_id=1, source_target_pairs={{0,16},{16,32},{32,48},{48,64},{64,80},{80,96},{96,112},{112,128},... | collective-permute-start | bytes 49160 | tf_op jit(solution)/shard_map/while/body/eval_jaxpr/ppermute | solution.py:12
  290.7 7.8 %collective-permute-start = (f32[16,256]{1,0:T(8,128)S(1)}, f32[16,256]{1,0:T(8,128)S(1)}, u32[]{:S(2)}, u32[]{:S(2)}) collective-permute-start(f32[16,256]{1,0:T(8,128)S(1)} %multiply_add_fusion.3), channel_id=1, source_target_pairs={{0,16},{16,32},{32,48},{48,64},{64,80},{80,96},{96,112},{112,128},... | collective-permute-start | bytes 49160 | tf_op jit(solution)/shard_map/while/body/eval_jaxpr/ppermute | solution.py:12
  298.5 7.7 %collective-permute-start = (f32[16,256]{1,0:T(8,128)S(1)}, f32[16,256]{1,0:T(8,128)S(1)}, u32[]{:S(2)}, u32[]{:S(2)}) collective-permute-start(f32[16,256]{1,0:T(8,128)S(1)} %multiply_add_fusion.3), channel_id=1, source_target_pairs={{0,16},{16,32},{32,48},{48,64},{64,80},{80,96},{96,112},{112,128},... | collective-permute-start | bytes 49160 | tf_op jit(solution)/shard_map/while/body/eval_jaxpr/ppermute | solution.py:12
  306.3 7.7 %collective-permute-start = (f32[16,256]{1,0:T(8,128)S(1)}, f32[16,256]{1,0:T(8,128)S(1)}, u32[]{:S(2)}, u32[]{:S(2)}) collective-permute-start(f32[16,256]{1,0:T(8,128)S(1)} %multiply_add_fusion.3), channel_id=1, source_target_pairs={{0,16},{16,32},{32,48},{48,64},{64,80},{80,96},{96,112},{112,128},... | collective-permute-start | bytes 49160 | tf_op jit(solution)/shard_map/while/body/eval_jaxpr/ppermute | solution.py:12
  314.0 7.7 %collective-permute-start = (f32[16,256]{1,0:T(8,128)S(1)}, f32[16,256]{1,0:T(8,128)S(1)}, u32[]{:S(2)}, u32[]{:S(2)}) collective-permute-start(f32[16,256]{1,0:T(8,128)S(1)} %multiply_add_fusion.3), channel_id=1, source_target_pairs={{0,16},{16,32},{32,48},{48,64},{64,80},{80,96},{96,112},{112,128},... | collective-permute-start | bytes 49160 | tf_op jit(solution)/shard_map/while/body/eval_jaxpr/ppermute | solution.py:12
  321.7 7.7 %collective-permute-start = (f32[16,256]{1,0:T(8,128)S(1)}, f32[16,256]{1,0:T(8,128)S(1)}, u32[]{:S(2)}, u32[]{:S(2)}) collective-permute-start(f32[16,256]{1,0:T(8,128)S(1)} %multiply_add_fusion.3), channel_id=1, source_target_pairs={{0,16},{16,32},{32,48},{48,64},{64,80},{80,96},{96,112},{112,128},... | collective-permute-start | bytes 49160 | tf_op jit(solution)/shard_map/while/body/eval_jaxpr/ppermute | solution.py:12
  329.5 7.7 %collective-permute-start = (f32[16,256]{1,0:T(8,128)S(1)}, f32[16,256]{1,0:T(8,128)S(1)}, u32[]{:S(2)}, u32[]{:S(2)}) collective-permute-start(f32[16,256]{1,0:T(8,128)S(1)} %multiply_add_fusion.3), channel_id=1, source_target_pairs={{0,16},{16,32},{32,48},{48,64},{64,80},{80,96},{96,112},{112,128},... | collective-permute-start | bytes 49160 | tf_op jit(solution)/shard_map/while/body/eval_jaxpr/ppermute | solution.py:12
  337.2 7.9 %collective-permute-start = (f32[16,256]{1,0:T(8,128)S(1)}, f32[16,256]{1,0:T(8,128)S(1)}, u32[]{:S(2)}, u32[]{:S(2)}) collective-permute-start(f32[16,256]{1,0:T(8,128)S(1)} %multiply_add_fusion.3), channel_id=1, source_target_pairs={{0,16},{16,32},{32,48},{48,64},{64,80},{80,96},{96,112},{112,128},... | collective-permute-start | bytes 49160 | tf_op jit(solution)/shard_map/while/body/eval_jaxpr/ppermute | solution.py:12
  345.1 7.7 %collective-permute-start = (f32[16,256]{1,0:T(8,128)S(1)}, f32[16,256]{1,0:T(8,128)S(1)}, u32[]{:S(2)}, u32[]{:S(2)}) collective-permute-start(f32[16,256]{1,0:T(8,128)S(1)} %multiply_add_fusion.3), channel_id=1, source_target_pairs={{0,16},{16,32},{32,48},{48,64},{64,80},{80,96},{96,112},{112,128},... | collective-permute-start | bytes 49160 | tf_op jit(solution)/shard_map/while/body/eval_jaxpr/ppermute | solution.py:12
  352.9 7.7 %collective-permute-start = (f32[16,256]{1,0:T(8,128)S(1)}, f32[16,256]{1,0:T(8,128)S(1)}, u32[]{:S(2)}, u32[]{:S(2)}) collective-permute-start(f32[16,256]{1,0:T(8,128)S(1)} %multiply_add_fusion.3), channel_id=1, source_target_pairs={{0,16},{16,32},{32,48},{48,64},{64,80},{80,96},{96,112},{112,128},... | collective-permute-start | bytes 49160 | tf_op jit(solution)/shard_map/while/body/eval_jaxpr/ppermute | solution.py:12
  360.6 7.7 %collective-permute-start = (f32[16,256]{1,0:T(8,128)S(1)}, f32[16,256]{1,0:T(8,128)S(1)}, u32[]{:S(2)}, u32[]{:S(2)}) collective-permute-start(f32[16,256]{1,0:T(8,128)S(1)} %multiply_add_fusion.3), channel_id=1, source_target_pairs={{0,16},{16,32},{32,48},{48,64},{64,80},{80,96},{96,112},{112,128},... | collective-permute-start | bytes 49160 | tf_op jit(solution)/shard_map/while/body/eval_jaxpr/ppermute | solution.py:12
  368.3 7.7 %collective-permute-start = (f32[16,256]{1,0:T(8,128)S(1)}, f32[16,256]{1,0:T(8,128)S(1)}, u32[]{:S(2)}, u32[]{:S(2)}) collective-permute-start(f32[16,256]{1,0:T(8,128)S(1)} %multiply_add_fusion.3), channel_id=1, source_target_pairs={{0,16},{16,32},{32,48},{48,64},{64,80},{80,96},{96,112},{112,128},... | collective-permute-start | bytes 49160 | tf_op jit(solution)/shard_map/while/body/eval_jaxpr/ppermute | solution.py:12
  376.1 7.7 %collective-permute-start = (f32[16,256]{1,0:T(8,128)S(1)}, f32[16,256]{1,0:T(8,128)S(1)}, u32[]{:S(2)}, u32[]{:S(2)}) collective-permute-start(f32[16,256]{1,0:T(8,128)S(1)} %multiply_add_fusion.3), channel_id=1, source_target_pairs={{0,16},{16,32},{32,48},{48,64},{64,80},{80,96},{96,112},{112,128},... | collective-permute-start | bytes 49160 | tf_op jit(solution)/shard_map/while/body/eval_jaxpr/ppermute | solution.py:12
  383.8 7.9 %collective-permute-start = (f32[16,256]{1,0:T(8,128)S(1)}, f32[16,256]{1,0:T(8,128)S(1)}, u32[]{:S(2)}, u32[]{:S(2)}) collective-permute-start(f32[16,256]{1,0:T(8,128)S(1)} %multiply_add_fusion.3), channel_id=1, source_target_pairs={{0,16},{16,32},{32,48},{48,64},{64,80},{80,96},{96,112},{112,128},... | collective-permute-start | bytes 49160 | tf_op jit(solution)/shard_map/while/body/eval_jaxpr/ppermute | solution.py:12
  391.7 7.7 %collective-permute-start = (f32[16,256]{1,0:T(8,128)S(1)}, f32[16,256]{1,0:T(8,128)S(1)}, u32[]{:S(2)}, u32[]{:S(2)}) collective-permute-start(f32[16,256]{1,0:T(8,128)S(1)} %multiply_add_fusion.3), channel_id=1, source_target_pairs={{0,16},{16,32},{32,48},{48,64},{64,80},{80,96},{96,112},{112,128},... | collective-permute-start | bytes 49160 | tf_op jit(solution)/shard_map/while/body/eval_jaxpr/ppermute | solution.py:12
  399.4 7.7 %collective-permute-start = (f32[16,256]{1,0:T(8,128)S(1)}, f32[16,256]{1,0:T(8,128)S(1)}, u32[]{:S(2)}, u32[]{:S(2)}) collective-permute-start(f32[16,256]{1,0:T(8,128)S(1)} %multiply_add_fusion.3), channel_id=1, source_target_pairs={{0,16},{16,32},{32,48},{48,64},{64,80},{80,96},{96,112},{112,128},... | collective-permute-start | bytes 49160 | tf_op jit(solution)/shard_map/while/body/eval_jaxpr/ppermute | solution.py:12
  407.2 7.7 %collective-permute-start = (f32[16,256]{1,0:T(8,128)S(1)}, f32[16,256]{1,0:T(8,128)S(1)}, u32[]{:S(2)}, u32[]{:S(2)}) collective-permute-start(f32[16,256]{1,0:T(8,128)S(1)} %multiply_add_fusion.3), channel_id=1, source_target_pairs={{0,16},{16,32},{32,48},{48,64},{64,80},{80,96},{96,112},{112,128},... | collective-permute-start | bytes 49160 | tf_op jit(solution)/shard_map/while/body/eval_jaxpr/ppermute | solution.py:12
  414.9 7.7 %collective-permute-start = (f32[16,256]{1,0:T(8,128)S(1)}, f32[16,256]{1,0:T(8,128)S(1)}, u32[]{:S(2)}, u32[]{:S(2)}) collective-permute-start(f32[16,256]{1,0:T(8,128)S(1)} %multiply_add_fusion.3), channel_id=1, source_target_pairs={{0,16},{16,32},{32,48},{48,64},{64,80},{80,96},{96,112},{112,128},... | collective-permute-start | bytes 49160 | tf_op jit(solution)/shard_map/while/body/eval_jaxpr/ppermute | solution.py:12
  422.6 7.7 %collective-permute-start = (f32[16,256]{1,0:T(8,128)S(1)}, f32[16,256]{1,0:T(8,128)S(1)}, u32[]{:S(2)}, u32[]{:S(2)}) collective-permute-start(f32[16,256]{1,0:T(8,128)S(1)} %multiply_add_fusion.3), channel_id=1, source_target_pairs={{0,16},{16,32},{32,48},{48,64},{64,80},{80,96},{96,112},{112,128},... | collective-permute-start | bytes 49160 | tf_op jit(solution)/shard_map/while/body/eval_jaxpr/ppermute | solution.py:12
  430.4 7.9 %collective-permute-start = (f32[16,256]{1,0:T(8,128)S(1)}, f32[16,256]{1,0:T(8,128)S(1)}, u32[]{:S(2)}, u32[]{:S(2)}) collective-permute-start(f32[16,256]{1,0:T(8,128)S(1)} %multiply_add_fusion.3), channel_id=1, source_target_pairs={{0,16},{16,32},{32,48},{48,64},{64,80},{80,96},{96,112},{112,128},... | collective-permute-start | bytes 49160 | tf_op jit(solution)/shard_map/while/body/eval_jaxpr/ppermute | solution.py:12
  438.2 7.7 %collective-permute-start = (f32[16,256]{1,0:T(8,128)S(1)}, f32[16,256]{1,0:T(8,128)S(1)}, u32[]{:S(2)}, u32[]{:S(2)}) collective-permute-start(f32[16,256]{1,0:T(8,128)S(1)} %multiply_add_fusion.3), channel_id=1, source_target_pairs={{0,16},{16,32},{32,48},{48,64},{64,80},{80,96},{96,112},{112,128},... | collective-permute-start | bytes 49160 | tf_op jit(solution)/shard_map/while/body/eval_jaxpr/ppermute | solution.py:12
  446.0 7.7 %collective-permute-start = (f32[16,256]{1,0:T(8,128)S(1)}, f32[16,256]{1,0:T(8,128)S(1)}, u32[]{:S(2)}, u32[]{:S(2)}) collective-permute-start(f32[16,256]{1,0:T(8,128)S(1)} %multiply_add_fusion.3), channel_id=1, source_target_pairs={{0,16},{16,32},{32,48},{48,64},{64,80},{80,96},{96,112},{112,128},... | collective-permute-start | bytes 49160 | tf_op jit(solution)/shard_map/while/body/eval_jaxpr/ppermute | solution.py:12
  453.7 7.7 %collective-permute-start = (f32[16,256]{1,0:T(8,128)S(1)}, f32[16,256]{1,0:T(8,128)S(1)}, u32[]{:S(2)}, u32[]{:S(2)}) collective-permute-start(f32[16,256]{1,0:T(8,128)S(1)} %multiply_add_fusion.3), channel_id=1, source_target_pairs={{0,16},{16,32},{32,48},{48,64},{64,80},{80,96},{96,112},{112,128},... | collective-permute-start | bytes 49160 | tf_op jit(solution)/shard_map/while/body/eval_jaxpr/ppermute | solution.py:12
  461.5 7.7 %collective-permute-start = (f32[16,256]{1,0:T(8,128)S(1)}, f32[16,256]{1,0:T(8,128)S(1)}, u32[]{:S(2)}, u32[]{:S(2)}) collective-permute-start(f32[16,256]{1,0:T(8,128)S(1)} %multiply_add_fusion.3), channel_id=1, source_target_pairs={{0,16},{16,32},{32,48},{48,64},{64,80},{80,96},{96,112},{112,128},... | collective-permute-start | bytes 49160 | tf_op jit(solution)/shard_map/while/body/eval_jaxpr/ppermute | solution.py:12
  469.2 7.7 %collective-permute-start = (f32[16,256]{1,0:T(8,128)S(1)}, f32[16,256]{1,0:T(8,128)S(1)}, u32[]{:S(2)}, u32[]{:S(2)}) collective-permute-start(f32[16,256]{1,0:T(8,128)S(1)} %multiply_add_fusion.3), channel_id=1, source_target_pairs={{0,16},{16,32},{32,48},{48,64},{64,80},{80,96},{96,112},{112,128},... | collective-permute-start | bytes 49160 | tf_op jit(solution)/shard_map/while/body/eval_jaxpr/ppermute | solution.py:12
  476.9 4.7 copy-start.4
  476.9 5.6 copy-start.14
  476.9 5.6 copy-start.15
  478.2 7.2 copy-start.1
  482.9 264.7 %copy-start.3 = (bf16[16,2048]{1,0:T(8,128)(2,1)S(1)}, bf16[16,2048]{1,0:T(8,128)(2,1)}, u32[]{:S(2)}) copy-start(bf16[16,2048]{1,0:T(8,128)(2,1)} %param.17) | copy-start | bytes 196612
  483.9 263.6 %reduce-scatter.3.cloned.1.call-start = ((), (), s32[]{:S(2)}) async-start(), calls=%async_computation.3 | async-start | bytes 2228224 | tf_op jit(solution)/shard_map/reduce_scatter | solution.py:151
Sparse Core Ops, SparseCore 0:
  10.7 46.5 all-gather.1
  66.9 108.1 all-reduce.22
  484.1 198.4 all-reduce.24
  685.2 62.3 reduce-scatter.2
where the time goes:
time: 760 us; the launch traced here: 756 us
  waiting for transfers between devices  290 us (38%)
  starting transfers between devices  191 us (25%)
  blocking collectives  161 us (21%)
  other arithmetic  52.1 us (7%)
  local copies, waits for them, and re-layouts  38.7 us (5%)
  between operations  14.9 us (2%)
    ppermute x32, starting transfers between devices, shifted(): return lax.ppermute(block, axis, route)  191 us
    unnamed x1, blocking collectives  161 us
    psum x1, waiting for transfers between devices, on_device(): lax.psum(jnp.dot(activated, w_x, preferred_element_type=jnp.float32), 'ch...  107 us
    reduce_scatter x1, waiting for transfers between devices, on_device(): lax.psum_scatter(jnp.dot(switched_result, w_out, preferred_element_type=j...  63.7 us
    ppermute x32, waiting for transfers between devices, shifted(): return lax.ppermute(block, axis, route)  47.9 us
    all_gather x1, waiting for transfers between devices, on_device(): lax.all_gather(rescaled_entries, 'chan', axis=0, tiled=True)  42.3 us
    unnamed x5, waiting for transfers between devices  29.2 us
  transfers between devices with their start and end apart: 36, of which 36 were waited for; matrix products, arithmetic and copies ran while one was open for 2% of the time, Pallas kernels for 0%

commit v1 on v0

--- a/solution.py
+++ b/solution.py
@@ -87,7 +87,9 @@
             + conv_weight[lower][None, :] * extended[lower : lower + seq_rows] * same_req[:, None]
         )
     activated = jax.nn.silu(conv_sum).astype(jnp.bfloat16)
-    x_proj = lax.psum(jnp.dot(activated, w_x, preferred_element_type=jnp.float32), "chan")
+    x_proj = jnp.sum(
+        lax.all_gather(jnp.dot(activated, w_x, preferred_element_type=jnp.float32), "chan"), axis=0
+    )
     thin_timescale_factor = x_proj[:, :rank_size].astype(jnp.bfloat16)
     in_coef = x_proj[:, rank_size : rank_size + state_size]
     out_coef = x_proj[:, rank_size + state_size :]

time: 760 us -> 694 us (0.913)
  the two profiles are of different devices: /device:TPU:4 before, /device:TPU:2 now
where the time goes in v1:
time: 694 us; the launch traced here: 689 us
  waiting for transfers between devices  223 us (32%)
  starting transfers between devices  187 us (27%)
  blocking collectives  165 us (24%)
  other arithmetic  52 us (7%)
  local copies, waits for them, and re-layouts  39.9 us (6%)
  between operations  15 us (2%)
    ppermute x32, starting transfers between devices, shifted(): return lax.ppermute(block, axis, route)  187 us
    unnamed x1, blocking collectives  165 us
    reduce_scatter x1, waiting for transfers between devices, on_device(): lax.psum_scatter(jnp.dot(switched_result, w_out, preferred_element_type=j...  63.4 us
    ppermute x32, waiting for transfers between devices, shifted(): return lax.ppermute(block, axis, route)  49.1 us
    all_gather x1, waiting for transfers between devices, on_device(): lax.all_gather(rescaled_entries, 'chan', axis=0, tiled=True)  43.1 us
    all_gather x1, waiting for transfers between devices, on_device(): lax.all_gather(jnp.dot(activated, w_x, preferred_element_type=jnp.float32...  40.4 us
    unnamed x5, waiting for transfers between devices  26.8 us
  transfers between devices with their start and end apart: 36, of which 36 were waited for; matrix products, arithmetic and copies ran while one was open for 2% of the time, Pallas kernels for 0%

profile of v1, /device:TPU:2, one launch (start us, length us, event | category | flops | bytes accessed | tf_op | source)
XLA Modules:
  0.0 689.4 jit_solution(10490676863791313917)
XLA Ops:
  8.4 1.6 fusion.22
  14.2 43.1 %all-gather.4.cloned.1.call-done = bf16[256,2048]{1,0:T(8,128)(2,1)} async-done(((bf16[16,2048]{1,0:T(8,128)(2,1)}), bf16[256,2048]{1,0:T(8,128)(2,1)}) %all-gather.4.cloned.1.call-update) | async-done | bytes 1048592 | tf_op jit(solution)/shard_map/all_gather | solution.py:71
  57.3 1.9 convolution_bitcast_fusion
  59.3 3.4 collective-permute-start.1
  62.8 2.0 collective-permute-done.1
  68.1 40.4 %all-gather.6.cloned.1.call-done = f32[4096,160]{0,1:T(8,128)} async-done(((f32[256,160]{0,1:T(8,128)}), f32[4096,160]{0,1:T(8,128)}) %all-gather.6.cloned.1.call-update) | async-done | bytes 2621456 | tf_op jit(solution)/shard_map/all_gather | solution.py:91
  108.6 2.7 copy.49
  113.3 49.4 %while.28 = (s32[]{:T(128)}, f32[16,16,256]{2,1,0:T(8,128)S(1)}, f32[16,16,256]{2,1,0:T(8,128)S(1)}, f32[16,16,256]{2,1,0:T(8,128)}, f32[16,16,16,256]{3,2,1,0:T...) while((s32[]{:T(128)}, f32[16,16,256]{2,1,0:T(8,128)S(1)}, ...), condition=%wide.region_9.10_spmd.clone, body=%wide.region_7.9_spmd.clone.sunk | while | flops 851971 | bytes 1532312 | solution.py:128
  169.5 2.9 pad.59
  172.5 1.6 pad_maximum_fusion
  174.0 2.9 pad.58
  177.7 231.3 %while.27 = (s32[]{:T(128)}, f32[16,256]{1,0:T(8,128)S(1)}, f32[16,256]{1,0:T(8,128)S(1)}, f32[16,256]{1,0:T(8,128)S(1)}, s32[]{:T(128)}) while((s32[]{:T(128)}, f32[16,256]{1,0:T(8,128)S(1)}, f32[16,256]{1,0:T(8,128)S(1)}, f32[16,256]{1,0:T(8,128)S(1)}, s32[]{:T(128)}) %tuple.80), condition=%wide.region_11.12_spmd, body=%wide.region_10.11_spmd.sunk | while | flops 8194 | bytes 131173 | solution.py:138
  177.7 3.4 collective-permute-start
  181.1 2.2 collective-permute-done
  183.3 3.4 collective-permute-start
  186.7 2.2 collective-permute-done
  188.9 3.4 collective-permute-start
  192.3 2.2 collective-permute-done
  194.6 3.5 collective-permute-start
  198.1 2.1 collective-permute-done
  200.2 5.6 collective-permute-start
  205.8 1.4 collective-permute-done
  207.3 6.3 collective-permute-start
  213.6 1.4 collective-permute-done
  215.0 6.3 collective-permute-start
  221.3 1.4 collective-permute-done
  222.7 6.3 collective-permute-start
  230.5 6.4 collective-permute-start
  236.9 1.4 collective-permute-done
  238.3 6.3 collective-permute-start
  246.0 6.3 collective-permute-start
  252.4 1.4 collective-permute-done
  253.8 6.3 collective-permute-start
  261.5 6.3 collective-permute-start
  267.8 1.4 collective-permute-done
  269.3 6.3 collective-permute-start
  275.6 1.4 collective-permute-done
  277.0 6.5 collective-permute-start
  283.5 1.4 collective-permute-done
  284.9 6.3 collective-permute-start
  291.2 1.4 collective-permute-done
  292.6 6.3 collective-permute-start
  300.4 6.3 collective-permute-start
  306.7 1.4 collective-permute-done
  308.1 6.3 collective-permute-start
  314.4 1.4 collective-permute-done
  315.8 6.3 collective-permute-start
  323.6 6.4 collective-permute-start
  331.5 6.3 collective-permute-start
  339.2 6.3 collective-permute-start
  346.9 6.3 collective-permute-start
  354.7 6.3 collective-permute-start
  362.4 6.3 collective-permute-start
  370.1 6.4 collective-permute-start
  378.0 6.3 collective-permute-start
  385.8 6.3 collective-permute-start
  393.5 6.3 collective-permute-start
  401.2 6.3 collective-permute-start
  410.2 3.3 multiply_reduce_fusion.1
  417.4 1.8 fusion.54
  423.8 165.4 %all-reduce.19 = bf16[4,4,256]{2,1,0:T(4,128)(2,1)S(1)} all-reduce(f32[4,4,256]{2,1,0:T(4,128)S(1)} %fusion.25), channel_id=5, replica_groups=mesh['seq'=32,'chan'=16] {'seq'}, use_global_device_ids=true, to_apply=%region_16.17.clone | all-reduce | flops 4096 | bytes 24576
  589.9 26.7 %all-reduce.22.cloned.1.call-done = f32[4,16,256]{1,0,2:T(4,128)} async-done(((f32[4,16,256]{1,0,2:T(4,128)}), f32[4,16,256]{1,0,2:T(4,128)}) %all-reduce.22.cloned.1.call-update) | async-done | bytes 65552
  617.9 63.4 %reduce-scatter.3.cloned.1.call-done = f32[16,2048]{1,0:T(8,128)} async-done(((f32[256,2048]{1,0:T(8,128)}), f32[16,2048]{1,0:T(8,128)}) %reduce-scatter.3.cloned.1.call-update) | async-done | bytes 131088 | tf_op jit(solution)/shard_map/reduce_scatter | solution.py:153
  681.4 1.6 fusion.23
  (292 shorter events, 101.1 us)
Async XLA Ops:
  7.2 50.1 %copy-start = (bf16[2,2048,256]{2,1,0:T(8,128)(2,1)S(1)}, bf16[2,2048,256]{2,1,0:T(8,128)(2,1)}, u32[]{:S(2)}) copy-start(bf16[2,2048,256]{2,1,0:T(8,128)(2,1)} %param.19) | copy-start | bytes 6291460
  7.2 57.7 %copy-start.13 = (f32[256]{0:T(256)S(1)}, f32[256]{0:T(256)}, u32[]{:S(2)}) copy-start(f32[256]{0:T(256)} %param.21) | copy-start | bytes 3076
  7.2 57.9 %copy-start.5 = (bf16[256,160]{0,1:T(8,128)(2,1)S(1)}, bf16[256,160]{0,1:T(8,128)(2,1)}, u32[]{:S(2)}) copy-start(bf16[256,160]{0,1:T(8,128)(2,1)} %param.22) | copy-start | bytes 245764
  7.2 60.1 %copy-start.6 = (f32[16,256]{1,0:T(8,128)S(1)}, f32[16,256]{1,0:T(8,128)}, u32[]{:S(2)}) copy-start(f32[16,256]{1,0:T(8,128)} %param.25) | copy-start | bytes 49156
  7.2 50.1 %all-gather.4.cloned.1.call-start = ((), (), s32[]{:S(2)}) async-start(), calls=%async_computation.1 | async-start | bytes 1114112 | tf_op jit(solution)/shard_map/all_gather | solution.py:71
  10.0 98.6 %all-gather.6.cloned.1.call-start = ((), (), s32[]{:S(2)}) async-start(), calls=%async_computation.3 | async-start | bytes 2785280 | tf_op jit(solution)/shard_map/all_gather | solution.py:91
  13.1 53.7 %copy-start.14 = (s32[4]{0:T(128)}, s32[4]{0:T(128)S(1)}, u32[]{:S(2)}) copy-start(s32[4]{0:T(128)S(1)} %get-tuple-element.173) | copy-start | bytes 52
  14.2 52.0 %copy-start.9 = (f32[1,256]{1,0:T(1,128)}, f32[1,256]{1,0:T(1,128)S(1)}, u32[]{:S(2)}) copy-start(f32[1,256]{1,0:T(1,128)S(1)} %get-tuple-element.233) | copy-start | bytes 3076
  14.2 52.0 %copy-start.10 = (f32[1,256]{1,0:T(1,128)}, f32[1,256]{1,0:T(1,128)S(1)}, u32[]{:S(2)}) copy-start(f32[1,256]{1,0:T(1,128)S(1)} %get-tuple-element.234) | copy-start | bytes 3076
  14.2 52.0 %copy-start.11 = (f32[1,256]{1,0:T(1,128)}, f32[1,256]{1,0:T(1,128)S(1)}, u32[]{:S(2)}) copy-start(f32[1,256]{1,0:T(1,128)S(1)} %get-tuple-element.235) | copy-start | bytes 3076
  14.2 52.0 %copy-start.12 = (f32[1,256]{1,0:T(1,128)}, f32[1,256]{1,0:T(1,128)S(1)}, u32[]{:S(2)}) copy-start(f32[1,256]{1,0:T(1,128)S(1)} %get-tuple-element.236) | copy-start | bytes 3076
  59.2 5.6 copy-start.2
  59.3 5.5 collective-permute-start.1
  62.8 3.4 copy-start.7
  62.8 3.4 copy-start.8
  66.0 550.6 %all-reduce.22.cloned.1.call-start = ((), (), s32[]{:S(2)}) async-start(), calls=%async_computation.4 | async-start | bytes 1048576
  67.4 44.3 %copy-start.17 = (bf16[128,256]{1,0:T(8,128)(2,1)S(1)}, bf16[128,256]{1,0:T(8,128)(2,1)}, u32[]{:S(2)}) copy-start(bf16[128,256]{1,0:T(8,128)(2,1)} %param.23) | copy-start | bytes 196612
  67.4 44.3 %copy-start.18 = (f32[256]{0:T(256)S(1)}, f32[256]{0:T(256)}, u32[]{:S(2)}) copy-start(f32[256]{0:T(256)} %param.24) | copy-start | bytes 3076
  177.7 5.6 collective-permute-start
  183.3 5.6 collective-permute-start
  188.9 5.6 collective-permute-start
  194.6 5.6 collective-permute-start
  200.2 7.1 %collective-permute-start = (f32[16,256]{1,0:T(8,128)S(1)}, f32[16,256]{1,0:T(8,128)S(1)}, u32[]{:S(2)}, u32[]{:S(2)}) collective-permute-start(f32[16,256]{1,0:T(8,128)S(1)} %multiply_add_fusion.3), channel_id=1, source_target_pairs={{0,16},{16,32},{32,48},{48,64},{64,80},{80,96},{96,112},{112,128},... | collective-permute-start | bytes 49160 | tf_op jit(solution)/shard_map/while/body/eval_jaxpr/ppermute | solution.py:12
  207.3 7.7 %collective-permute-start = (f32[16,256]{1,0:T(8,128)S(1)}, f32[16,256]{1,0:T(8,128)S(1)}, u32[]{:S(2)}, u32[]{:S(2)}) collective-permute-start(f32[16,256]{1,0:T(8,128)S(1)} %multiply_add_fusion.3), channel_id=1, source_target_pairs={{0,16},{16,32},{32,48},{48,64},{64,80},{80,96},{96,112},{112,128},... | collective-permute-start | bytes 49160 | tf_op jit(solution)/shard_map/while/body/eval_jaxpr/ppermute | solution.py:12
  215.0 7.7 %collective-permute-start = (f32[16,256]{1,0:T(8,128)S(1)}, f32[16,256]{1,0:T(8,128)S(1)}, u32[]{:S(2)}, u32[]{:S(2)}) collective-permute-start(f32[16,256]{1,0:T(8,128)S(1)} %multiply_add_fusion.3), channel_id=1, source_target_pairs={{0,16},{16,32},{32,48},{48,64},{64,80},{80,96},{96,112},{112,128},... | collective-permute-start | bytes 49160 | tf_op jit(solution)/shard_map/while/body/eval_jaxpr/ppermute | solution.py:12
  222.7 7.7 %collective-permute-start = (f32[16,256]{1,0:T(8,128)S(1)}, f32[16,256]{1,0:T(8,128)S(1)}, u32[]{:S(2)}, u32[]{:S(2)}) collective-permute-start(f32[16,256]{1,0:T(8,128)S(1)} %multiply_add_fusion.3), channel_id=1, source_target_pairs={{0,16},{16,32},{32,48},{48,64},{64,80},{80,96},{96,112},{112,128},... | collective-permute-start | bytes 49160 | tf_op jit(solution)/shard_map/while/body/eval_jaxpr/ppermute | solution.py:12
  230.5 7.8 %collective-permute-start = (f32[16,256]{1,0:T(8,128)S(1)}, f32[16,256]{1,0:T(8,128)S(1)}, u32[]{:S(2)}, u32[]{:S(2)}) collective-permute-start(f32[16,256]{1,0:T(8,128)S(1)} %multiply_add_fusion.3), channel_id=1, source_target_pairs={{0,16},{16,32},{32,48},{48,64},{64,80},{80,96},{96,112},{112,128},... | collective-permute-start | bytes 49160 | tf_op jit(solution)/shard_map/while/body/eval_jaxpr/ppermute | solution.py:12
  238.3 7.7 %collective-permute-start = (f32[16,256]{1,0:T(8,128)S(1)}, f32[16,256]{1,0:T(8,128)S(1)}, u32[]{:S(2)}, u32[]{:S(2)}) collective-permute-start(f32[16,256]{1,0:T(8,128)S(1)} %multiply_add_fusion.3), channel_id=1, source_target_pairs={{0,16},{16,32},{32,48},{48,64},{64,80},{80,96},{96,112},{112,128},... | collective-permute-start | bytes 49160 | tf_op jit(solution)/shard_map/while/body/eval_jaxpr/ppermute | solution.py:12
  246.0 7.7 %collective-permute-start = (f32[16,256]{1,0:T(8,128)S(1)}, f32[16,256]{1,0:T(8,128)S(1)}, u32[]{:S(2)}, u32[]{:S(2)}) collective-permute-start(f32[16,256]{1,0:T(8,128)S(1)} %multiply_add_fusion.3), channel_id=1, source_target_pairs={{0,16},{16,32},{32,48},{48,64},{64,80},{80,96},{96,112},{112,128},... | collective-permute-start | bytes 49160 | tf_op jit(solution)/shard_map/while/body/eval_jaxpr/ppermute | solution.py:12
  253.8 7.7 %collective-permute-start = (f32[16,256]{1,0:T(8,128)S(1)}, f32[16,256]{1,0:T(8,128)S(1)}, u32[]{:S(2)}, u32[]{:S(2)}) collective-permute-start(f32[16,256]{1,0:T(8,128)S(1)} %multiply_add_fusion.3), channel_id=1, source_target_pairs={{0,16},{16,32},{32,48},{48,64},{64,80},{80,96},{96,112},{112,128},... | collective-permute-start | bytes 49160 | tf_op jit(solution)/shard_map/while/body/eval_jaxpr/ppermute | solution.py:12
  261.5 7.7 %collective-permute-start = (f32[16,256]{1,0:T(8,128)S(1)}, f32[16,256]{1,0:T(8,128)S(1)}, u32[]{:S(2)}, u32[]{:S(2)}) collective-permute-start(f32[16,256]{1,0:T(8,128)S(1)} %multiply_add_fusion.3), channel_id=1, source_target_pairs={{0,16},{16,32},{32,48},{48,64},{64,80},{80,96},{96,112},{112,128},... | collective-permute-start | bytes 49160 | tf_op jit(solution)/shard_map/while/body/eval_jaxpr/ppermute | solution.py:12
  269.3 7.7 %collective-permute-start = (f32[16,256]{1,0:T(8,128)S(1)}, f32[16,256]{1,0:T(8,128)S(1)}, u32[]{:S(2)}, u32[]{:S(2)}) collective-permute-start(f32[16,256]{1,0:T(8,128)S(1)} %multiply_add_fusion.3), channel_id=1, source_target_pairs={{0,16},{16,32},{32,48},{48,64},{64,80},{80,96},{96,112},{112,128},... | collective-permute-start | bytes 49160 | tf_op jit(solution)/shard_map/while/body/eval_jaxpr/ppermute | solution.py:12
  277.0 7.9 %collective-permute-start = (f32[16,256]{1,0:T(8,128)S(1)}, f32[16,256]{1,0:T(8,128)S(1)}, u32[]{:S(2)}, u32[]{:S(2)}) collective-permute-start(f32[16,256]{1,0:T(8,128)S(1)} %multiply_add_fusion.3), channel_id=1, source_target_pairs={{0,16},{16,32},{32,48},{48,64},{64,80},{80,96},{96,112},{112,128},... | collective-permute-start | bytes 49160 | tf_op jit(solution)/shard_map/while/body/eval_jaxpr/ppermute | solution.py:12
  284.9 7.7 %collective-permute-start = (f32[16,256]{1,0:T(8,128)S(1)}, f32[16,256]{1,0:T(8,128)S(1)}, u32[]{:S(2)}, u32[]{:S(2)}) collective-permute-start(f32[16,256]{1,0:T(8,128)S(1)} %multiply_add_fusion.3), channel_id=1, source_target_pairs={{0,16},{16,32},{32,48},{48,64},{64,80},{80,96},{96,112},{112,128},... | collective-permute-start | bytes 49160 | tf_op jit(solution)/shard_map/while/body/eval_jaxpr/ppermute | solution.py:12
  292.6 7.7 %collective-permute-start = (f32[16,256]{1,0:T(8,128)S(1)}, f32[16,256]{1,0:T(8,128)S(1)}, u32[]{:S(2)}, u32[]{:S(2)}) collective-permute-start(f32[16,256]{1,0:T(8,128)S(1)} %multiply_add_fusion.3), channel_id=1, source_target_pairs={{0,16},{16,32},{32,48},{48,64},{64,80},{80,96},{96,112},{112,128},... | collective-permute-start | bytes 49160 | tf_op jit(solution)/shard_map/while/body/eval_jaxpr/ppermute | solution.py:12
  300.4 7.7 %collective-permute-start = (f32[16,256]{1,0:T(8,128)S(1)}, f32[16,256]{1,0:T(8,128)S(1)}, u32[]{:S(2)}, u32[]{:S(2)}) collective-permute-start(f32[16,256]{1,0:T(8,128)S(1)} %multiply_add_fusion.3), channel_id=1, source_target_pairs={{0,16},{16,32},{32,48},{48,64},{64,80},{80,96},{96,112},{112,128},... | collective-permute-start | bytes 49160 | tf_op jit(solution)/shard_map/while/body/eval_jaxpr/ppermute | solution.py:12
  308.1 7.7 %collective-permute-start = (f32[16,256]{1,0:T(8,128)S(1)}, f32[16,256]{1,0:T(8,128)S(1)}, u32[]{:S(2)}, u32[]{:S(2)}) collective-permute-start(f32[16,256]{1,0:T(8,128)S(1)} %multiply_add_fusion.3), channel_id=1, source_target_pairs={{0,16},{16,32},{32,48},{48,64},{64,80},{80,96},{96,112},{112,128},... | collective-permute-start | bytes 49160 | tf_op jit(solution)/shard_map/while/body/eval_jaxpr/ppermute | solution.py:12
  315.8 7.7 %collective-permute-start = (f32[16,256]{1,0:T(8,128)S(1)}, f32[16,256]{1,0:T(8,128)S(1)}, u32[]{:S(2)}, u32[]{:S(2)}) collective-permute-start(f32[16,256]{1,0:T(8,128)S(1)} %multiply_add_fusion.3), channel_id=1, source_target_pairs={{0,16},{16,32},{32,48},{48,64},{64,80},{80,96},{96,112},{112,128},... | collective-permute-start | bytes 49160 | tf_op jit(solution)/shard_map/while/body/eval_jaxpr/ppermute | solution.py:12
  323.6 7.9 %collective-permute-start = (f32[16,256]{1,0:T(8,128)S(1)}, f32[16,256]{1,0:T(8,128)S(1)}, u32[]{:S(2)}, u32[]{:S(2)}) collective-permute-start(f32[16,256]{1,0:T(8,128)S(1)} %multiply_add_fusion.3), channel_id=1, source_target_pairs={{0,16},{16,32},{32,48},{48,64},{64,80},{80,96},{96,112},{112,128},... | collective-permute-start | bytes 49160 | tf_op jit(solution)/shard_map/while/body/eval_jaxpr/ppermute | solution.py:12
  331.5 7.7 %collective-permute-start = (f32[16,256]{1,0:T(8,128)S(1)}, f32[16,256]{1,0:T(8,128)S(1)}, u32[]{:S(2)}, u32[]{:S(2)}) collective-permute-start(f32[16,256]{1,0:T(8,128)S(1)} %multiply_add_fusion.3), channel_id=1, source_target_pairs={{0,16},{16,32},{32,48},{48,64},{64,80},{80,96},{96,112},{112,128},... | collective-permute-start | bytes 49160 | tf_op jit(solution)/shard_map/while/body/eval_jaxpr/ppermute | solution.py:12
  339.2 7.7 %collective-permute-start = (f32[16,256]{1,0:T(8,128)S(1)}, f32[16,256]{1,0:T(8,128)S(1)}, u32[]{:S(2)}, u32[]{:S(2)}) collective-permute-start(f32[16,256]{1,0:T(8,128)S(1)} %multiply_add_fusion.3), channel_id=1, source_target_pairs={{0,16},{16,32},{32,48},{48,64},{64,80},{80,96},{96,112},{112,128},... | collective-permute-start | bytes 49160 | tf_op jit(solution)/shard_map/while/body/eval_jaxpr/ppermute | solution.py:12
  346.9 7.7 %collective-permute-start = (f32[16,256]{1,0:T(8,128)S(1)}, f32[16,256]{1,0:T(8,128)S(1)}, u32[]{:S(2)}, u32[]{:S(2)}) collective-permute-start(f32[16,256]{1,0:T(8,128)S(1)} %multiply_add_fusion.3), channel_id=1, source_target_pairs={{0,16},{16,32},{32,48},{48,64},{64,80},{80,96},{96,112},{112,128},... | collective-permute-start | bytes 49160 | tf_op jit(solution)/shard_map/while/body/eval_jaxpr/ppermute | solution.py:12
  354.7 7.7 %collective-permute-start = (f32[16,256]{1,0:T(8,128)S(1)}, f32[16,256]{1,0:T(8,128)S(1)}, u32[]{:S(2)}, u32[]{:S(2)}) collective-permute-start(f32[16,256]{1,0:T(8,128)S(1)} %multiply_add_fusion.3), channel_id=1, source_target_pairs={{0,16},{16,32},{32,48},{48,64},{64,80},{80,96},{96,112},{112,128},... | collective-permute-start | bytes 49160 | tf_op jit(solution)/shard_map/while/body/eval_jaxpr/ppermute | solution.py:12
  362.4 7.7 %collective-permute-start = (f32[16,256]{1,0:T(8,128)S(1)}, f32[16,256]{1,0:T(8,128)S(1)}, u32[]{:S(2)}, u32[]{:S(2)}) collective-permute-start(f32[16,256]{1,0:T(8,128)S(1)} %multiply_add_fusion.3), channel_id=1, source_target_pairs={{0,16},{16,32},{32,48},{48,64},{64,80},{80,96},{96,112},{112,128},... | collective-permute-start | bytes 49160 | tf_op jit(solution)/shard_map/while/body/eval_jaxpr/ppermute | solution.py:12
  370.1 7.9 %collective-permute-start = (f32[16,256]{1,0:T(8,128)S(1)}, f32[16,256]{1,0:T(8,128)S(1)}, u32[]{:S(2)}, u32[]{:S(2)}) collective-permute-start(f32[16,256]{1,0:T(8,128)S(1)} %multiply_add_fusion.3), channel_id=1, source_target_pairs={{0,16},{16,32},{32,48},{48,64},{64,80},{80,96},{96,112},{112,128},... | collective-permute-start | bytes 49160 | tf_op jit(solution)/shard_map/while/body/eval_jaxpr/ppermute | solution.py:12
  378.0 7.7 %collective-permute-start = (f32[16,256]{1,0:T(8,128)S(1)}, f32[16,256]{1,0:T(8,128)S(1)}, u32[]{:S(2)}, u32[]{:S(2)}) collective-permute-start(f32[16,256]{1,0:T(8,128)S(1)} %multiply_add_fusion.3), channel_id=1, source_target_pairs={{0,16},{16,32},{32,48},{48,64},{64,80},{80,96},{96,112},{112,128},... | collective-permute-start | bytes 49160 | tf_op jit(solution)/shard_map/while/body/eval_jaxpr/ppermute | solution.py:12
  385.8 7.7 %collective-permute-start = (f32[16,256]{1,0:T(8,128)S(1)}, f32[16,256]{1,0:T(8,128)S(1)}, u32[]{:S(2)}, u32[]{:S(2)}) collective-permute-start(f32[16,256]{1,0:T(8,128)S(1)} %multiply_add_fusion.3), channel_id=1, source_target_pairs={{0,16},{16,32},{32,48},{48,64},{64,80},{80,96},{96,112},{112,128},... | collective-permute-start | bytes 49160 | tf_op jit(solution)/shard_map/while/body/eval_jaxpr/ppermute | solution.py:12
  393.5 7.7 %collective-permute-start = (f32[16,256]{1,0:T(8,128)S(1)}, f32[16,256]{1,0:T(8,128)S(1)}, u32[]{:S(2)}, u32[]{:S(2)}) collective-permute-start(f32[16,256]{1,0:T(8,128)S(1)} %multiply_add_fusion.3), channel_id=1, source_target_pairs={{0,16},{16,32},{32,48},{48,64},{64,80},{80,96},{96,112},{112,128},... | collective-permute-start | bytes 49160 | tf_op jit(solution)/shard_map/while/body/eval_jaxpr/ppermute | solution.py:12
  401.2 7.7 %collective-permute-start = (f32[16,256]{1,0:T(8,128)S(1)}, f32[16,256]{1,0:T(8,128)S(1)}, u32[]{:S(2)}, u32[]{:S(2)}) collective-permute-start(f32[16,256]{1,0:T(8,128)S(1)} %multiply_add_fusion.3), channel_id=1, source_target_pairs={{0,16},{16,32},{32,48},{48,64},{64,80},{80,96},{96,112},{112,128},... | collective-permute-start | bytes 49160 | tf_op jit(solution)/shard_map/while/body/eval_jaxpr/ppermute | solution.py:12
  409.0 4.6 copy-start.4
  409.0 5.5 copy-start.15
  409.0 5.5 copy-start.16
  410.2 7.1 %copy-start.1 = (bf16[256,2048]{1,0:T(8,128)(2,1)S(1)}, bf16[256,2048]{1,0:T(8,128)(2,1)}, u32[]{:S(2)}) copy-start(bf16[256,2048]{1,0:T(8,128)(2,1)} %param.27) | copy-start | bytes 3145732
  414.9 266.5 %copy-start.3 = (bf16[16,2048]{1,0:T(8,128)(2,1)S(1)}, bf16[16,2048]{1,0:T(8,128)(2,1)}, u32[]{:S(2)}) copy-start(bf16[16,2048]{1,0:T(8,128)(2,1)} %param.17) | copy-start | bytes 196612
  415.9 265.4 %reduce-scatter.3.cloned.1.call-start = ((), (), s32[]{:S(2)}) async-start(), calls=%async_computation.2 | async-start | bytes 2228224 | tf_op jit(solution)/shard_map/reduce_scatter | solution.py:153
Sparse Core Ops, SparseCore 0:
  10.7 46.5 all-gather.3
  66.1 42.3 all-gather.5
  416.0 200.4 all-reduce.21
  619.3 62.0 reduce-scatter.2
